TPU v7x, 32 devices: a whole 2x2x4 slice. The times are simulated.
32 devices in a mesh: sub: 8 (over y, x, core), tm: 4 (over z).
Axes of the slice: x: 2, y: 2, z: 4, core: 2. Of those that a mesh axis runs over, the one named last changes fastest.
Arguments:
- voltages: bfloat16 [8192, 12, 2, 2048], P('sub', 'tm'), may hold values from -6 to 6
- slot_feed: int32 [2048], replicated, may hold values from 0 to 2047, each once
- chan_lag: int32 [8192], replicated, may hold values from 0 to 4096
- trial_dm: int32 [512], replicated, may hold values from 0 to 4096
- beam_order: int32 [1024], replicated, may hold values from 0 to 1023, each once
Outputs:
- dedispersed: float32 [1024, 12, 512], P('sub', 'tm')
Inputs may be any that keep to these rules, and one draw needn't show every extreme that they name: `slot_feed`: each feed once; slot (p * 4 + y) * 256 + n is polarization p at east-west position y and north-south position n. `beam_order`: each beam once.
All inputs are finite; a program needn't handle non-finite values.
Results may differ from a plain program's by a relative error of at most 0.00088.
Values may be sent and summed in bfloat16 or wider, within the bound.
No kernel may reach another device: no remote copies, remote signals or barrier semaphores. Data moves between devices by JAX's collectives and lax.ppermute only.
A program may use at most 192 MiB of HBM per device.

v0:
```python
import math
import jax
import jax.numpy as jnp
from jax import lax
from jax.sharding import PartitionSpec as P

NS = 256
CYL = 4
POL = 2
CHANNELS = 8192
NDM = 512
MAXD = 6
QUANT = 2796202


def shifted(value, axis, steps):
    count = lax.axis_size(axis)
    initial, last = (max(0, -steps), min(count, count - steps))
    return lax.ppermute(value, axis, [(source, source + steps) for source in range(initial, last)])


def north_table():
    positions = jnp.arange(NS, dtype=jnp.int32)
    phase_index = positions[:, None] * positions[None, :] % NS
    angles = phase_index.astype(jnp.float32) * (2.0 * math.pi / NS)
    cosine = jnp.cos(angles) / math.sqrt(NS)
    sine_part = jnp.sin(angles) / math.sqrt(NS)
    real_row = jnp.stack([cosine, -sine_part], axis=1)
    imag_row = jnp.stack([sine_part, cosine], axis=1)
    return jnp.stack([real_row, imag_row], axis=0).astype(jnp.bfloat16)


def west_table():
    cylinder = jnp.arange(CYL, dtype=jnp.int32)
    quarter_turn = cylinder[:, None] * cylinder[None, :] % 4
    cosine = (quarter_turn == 0).astype(jnp.float32) - (quarter_turn == 2).astype(jnp.float32)
    sine_part = (quarter_turn == 1).astype(jnp.float32) - (quarter_turn == 3).astype(jnp.float32)
    real_row = jnp.stack([cosine, -sine_part], axis=2)
    imag_row = jnp.stack([sine_part, cosine], axis=2)
    return 0.5 * jnp.stack([real_row, imag_row], axis=1)


def compute_power(north_beams):
    west_beams = jnp.einsum(
        "ctpyom,yoeq->ctpeqm", north_beams, west_table(), precision=lax.Precision.HIGHEST
    )
    squares = jnp.sum(west_beams * west_beams, axis=(2, 4))
    return squares.reshape(north_beams.shape[0], north_beams.shape[1], CYL * NS)


def delay_table(lag_rows, trial_dm):
    return lag_rows[:, None] * trial_dm[None, :] // QUANT


def shift_sum(source, delays, head_rows, out_rows):
    time_rows = source.shape[1]
    total_sum = jnp.zeros((source.shape[2], out_rows, NDM), jnp.float32)
    for delay_step in range(MAXD + 1):
        onehot = (delays == delay_step).astype(jnp.bfloat16)
        first_index = head_rows - delay_step
        begin_row = max(0, first_index)
        end_row = min(time_rows, first_index + out_rows)
        part = jnp.einsum("ctb,cd->btd", source, onehot, preferred_element_type=jnp.float32)
        front_pad = begin_row - first_index
        back_pad = out_rows - front_pad - (end_row - begin_row)
        total_sum = total_sum + jnp.pad(part, ((0, 0), (front_pad, back_pad), (0, 0)))
    return total_sum


def per_device(voltages, slot_feed, chan_lag, trial_dm, beam_order):
    channel_count = voltages.shape[0]
    sample_count = voltages.shape[1]
    shard_reach = (MAXD + sample_count - 1) // sample_count
    grid_volts = jnp.take(voltages, slot_feed, axis=3).reshape(
        channel_count, sample_count, 2, POL, CYL, NS
    )
    north_beams = jnp.einsum(
        "ctrpyn,rnom->ctpyom", grid_volts, north_table(), preferred_element_type=jnp.float32
    )
    intensity = compute_power(north_beams)
    ordered = jnp.take(intensity, beam_order, axis=2)
    totals = lax.psum(jnp.sum(ordered, axis=1), "tm")
    average = totals / (sample_count * lax.axis_size("tm"))
    normal = (ordered - average[:, None, :]).astype(jnp.bfloat16)
    head_rows = 0
    out_rows = sample_count + MAXD
    offset = lax.axis_index("sub") * channel_count
    lag_rows = lax.dynamic_slice_in_dim(chan_lag, offset, channel_count)
    delays = delay_table(lag_rows, trial_dm)
    result = lax.psum_scatter(
        shift_sum(normal, delays, head_rows, out_rows), "sub", scatter_dimension=0, tiled=True
    )
    kept_rows = result[:, :sample_count, :]
    for distance in range(1, shard_reach + 1):
        first_row = distance * sample_count
        last_row = min(first_row + sample_count, sample_count + MAXD)
        carried = shifted(result[:, first_row:last_row, :], "tm", distance)
        kept_rows = kept_rows + carried
    result = kept_rows
    return result / math.sqrt(CHANNELS)


def solution(mesh):
    return jax.shard_map(
        per_device,
        mesh=mesh,
        in_specs=(P("sub", "tm", None, None), P(), P(), P(), P()),
        out_specs=P("sub", "tm", None),
        check_vma=False,
    )
```

profile of v0, /device:TPU:24, one launch (start us, length us, event | category | flops | bytes accessed | tf_op | source)
XLA Modules:
  0.0 946.9 jit_solution(5524718804236857798)
XLA Ops:
  11.5 84.4 %copy.39 = bf16[1024,3,2,2048]{0,1,2,3:T(4,128)(2,1)} copy(bf16[1024,3,2,2048]{3,2,1,0:T(2,128)(2,1)} %param.5) | data formatting | bytes 50331648 | tf_op args[0]
  95.8 71.0 %gather_fusion = bf16[2048,1024,3,2]{1,2,3,0:T(4,128)(2,1)} fusion(bf16[1024,3,2,2048]{0,1,2,3:T(4,128)(2,1)} %copy.39, s32[2048]{0:T(1024)S(1)} %fusion.54), kind=kCustom, calls=%fused_computation | custom fusion | bytes 50339840 | tf_op jit(solution)/shard_map/jit(_take)/gather | solution.py:74
  166.9 48.4 %copy.40 = bf16[1024,3,2,2,4,256]{5,0,2,4,3,1:T(8,128)(2,1)} copy(bf16[1024,3,2,2,4,256]{0,1,2,5,4,3:T(4,128)(2,1)} %bitcast.98) | data formatting | bytes 50331648 | tf_op jit(solution)/shard_map/jit(_take)/gather | solution.py:74
  215.6 27.5 %fusion.8 = f32[1024,3,2,4,2,256]{5,0,4,3,2,1:T(8,128)} fusion(bf16[1024,3,2,2,4,256]{5,0,2,4,3,1:T(8,128)(2,1)} %copy.40, pred[2,4,256]{2,1,0:T(4,128)(4,1)S(1)} %broadcast_in_dim.34, bf16[1,256,2,256]{3,1,0,2:T(8,128)(2,1)S(1)} %get-tuple-element.8, bf16[1,256,2,256]{3,1,0,2:T(8,128)(2,1)S(1)} %get-tuple-element.7), kind=kOutput, calls=%fused_computation.11 | convolution fusion | flops 12898533376 | bytes 76023808 | tf_op jit(solution)/shard_map/ctrpyn,rnom->ctpyom/dot_general | solution.py:77
  243.0 186.1 %fusion = f32[4,1024,3,256]{3,0,2,1:T(4,128)} fusion(f32[1024,3,2,4,2,256]{5,0,4,3,2,1:T(8,128)} %fusion.8, f32[4,2,4,2,1,1,1]{0,2,1,6,5,4,3:T(4,128)S(1)} %fusion.107), kind=kOutput, calls=%fused_computation.3 | convolution fusion | flops 1229979648 | bytes 62914816 | tf_op jit(solution)/shard_map/ctpyom,yoeq->ctpeqm/dot_general | solution.py:44
  429.2 14.6 %copy.43 = f32[1024,3,4,256]{0,3,2,1:T(8,128)} copy(f32[1024,3,4,256]{3,2,1,0:T(4,128)} %bitcast.100) | data formatting | bytes 25165824 | tf_op jit(solution)/shard_map/reduce_sum | solution.py:47
  443.8 18.1 %copy.44 = f32[1024,3,1024]{0,1,2:T(4,128)} copy(f32[1024,3,1024]{0,2,1:T(8,128)} %bitcast.99) | data formatting | bytes 25165824 | tf_op jit(solution)/shard_map/reshape | solution.py:48
  461.8 26.0 %gather_fusion.1 = f32[1024,1024,3]{1,2,0:T(4,128)} fusion(f32[1024,3,1024]{0,1,2:T(4,128)} %copy.44, s32[1024]{0:T(1024)S(1)} %fusion.56), kind=kCustom, calls=%fused_computation.1 | custom fusion | bytes 25169920 | tf_op jit(solution)/shard_map/jit(_take)/gather | solution.py:81
  487.8 17.4 %copy.45 = f32[1024,1024,3]{0,1,2:T(8,128)} copy(f32[1024,1024,3]{1,2,0:T(4,128)} %gather_fusion.1) | data formatting | bytes 25165824 | tf_op jit(solution)/shard_map/jit(_take)/gather | solution.py:81
  505.2 8.8 bitcast_reduce_fusion
  514.9 152.9 %all-reduce.9.cloned.1.call-done = f32[1024,1024]{1,0:T(8,128)} async-done(((f32[1024,1024]{1,0:T(8,128)}), f32[1024,1024]{1,0:T(8,128)}) %all-reduce.9.cloned.1.call-update) | async-done | bytes 4194320 | tf_op jit(solution)/shard_map/psum | solution.py:82
  667.8 5.1 broadcast_multiply_fusion
  673.0 10.9 %fusion.11 = bf16[1024,3,1024]{2,0,1:T(8,128)(2,1)} fusion(f32[1024,1024,3]{0,1,2:T(8,128)} %copy.45, f32[1024,1024]{1,0:T(8,128)} %broadcast_multiply_fusion, pred[1024]{0:T(1024)(128)(4,1)S(1)} %compare_and_fusion.1), kind=kLoop, calls=%fused_computation.15 | loop fusion | flops 9437184 | bytes 23069696 | tf_op jit(solution)/shard_map/convert_element_type | solution.py:84
  683.9 7.8 convolution_bitcast_fusion.1
  691.7 5.3 convolution_bitcast_fusion.2
  697.0 7.2 convolution_bitcast_fusion.3
  704.1 7.3 convolution_bitcast_fusion.4
  711.4 7.2 convolution_bitcast_fusion.5
  718.6 7.1 convolution_bitcast_fusion.6
  725.8 7.6 convolution_bitcast_fusion
  733.3 20.4 %pad_add_fusion = f32[1024,9,512]{0,2,1:T(8,128)} fusion(f32[1024,3,512]{0,2,1:T(8,128)} %convolution_bitcast_fusion, f32[1024,3,512]{0,2,1:T(8,128)S(1)} %convolution_bitcast_fusion.1, f32[1024,3,512]{0,2,1:T(8,128)S(1)} %convolution_bitcast_fusion.2, f32[1024,3,512]{0,2,1:T(8,128)} %convolution_bitcast_fusion.3, ...), kind=kLoop, calls=%fused_computation.12 | loop fusion | flops 28311552 | bytes 62914560 | tf_op jit(solution)/shard_map/add | solution.py:66
  753.8 127.6 %reduce-scatter.2.cloned.1.call-done = f32[128,9,512]{0,2,1:T(8,128)} async-done(((f32[1024,9,512]{0,2,1:T(8,128)}), f32[128,9,512]{0,2,1:T(8,128)}) %reduce-scatter.2.cloned.1.call-update) | async-done | bytes 2359312 | tf_op jit(solution)/shard_map/reduce_scatter | solution.py:90
  885.4 18.8 %collective-permute-done = f32[128,3,512]{0,2,1:T(8,128)S(1)} collective-permute-done((f32[128,3,512]{0,2,1:T(8,128)S(1)}, f32[128,3,512]{0,2,1:T(8,128)S(1)}, u32[]{:S(2)}, u32[]{:S(2)}) %collective-permute-start) | collective-permute-done | bytes 786464 | tf_op jit(solution)/shard_map/ppermute | solution.py:19
  904.3 33.3 %collective-permute-done.1 = f32[128,3,512]{0,2,1:T(8,128)S(1)} collective-permute-done((f32[128,3,512]{0,2,1:T(8,128)S(1)}, f32[128,3,512]{0,2,1:T(8,128)S(1)}, u32[]{:S(2)}, u32[]{:S(2)}) %collective-permute-start.1) | collective-permute-done | bytes 786464 | tf_op jit(solution)/shard_map/ppermute | solution.py:19
  (28 shorter events, 12.6 us)
Async XLA Ops:
  6.5 661.3 %all-reduce.9.cloned.1.call-start = ((), (), s32[]{:S(2)}) async-start(), calls=%async_computation.1 | async-start | bytes 8388608 | tf_op jit(solution)/shard_map/psum | solution.py:82
  514.0 367.4 %reduce-scatter.2.cloned.1.call-start = ((), (), s32[]{:S(2)}) async-start(), calls=%async_computation.2 | async-start | bytes 21233664 | tf_op jit(solution)/shard_map/reduce_scatter | solution.py:90
  673.0 10.9 %copy-start.1 = (s32[512]{0:T(512)S(1)}, s32[512]{0:T(512)}, u32[]{:S(2)}) copy-start(s32[512]{0:T(512)} %param.8) | copy-start | bytes 6148
  683.9 7.8 copy-start
  882.8 21.4 %collective-permute-start = (f32[128,3,512]{0,2,1:T(8,128)S(1)}, f32[128,3,512]{0,2,1:T(8,128)S(1)}, u32[]{:S(2)}, u32[]{:S(2)}) collective-permute-start(f32[128,3,512]{0,2,1:T(8,128)S(1)} %get-tuple-element.5), channel_id=1, source_target_pairs={{0,1},{1,2},{2,3},{4,5},{5,6},{6,7},{8,9},{9,10},{10,11},{12,13},{... | collective-permute-start | bytes 2359304 | tf_op jit(solution)/shard_map/ppermute | solution.py:19
  884.1 53.4 %collective-permute-start.1 = (f32[128,3,512]{0,2,1:T(8,128)S(1)}, f32[128,3,512]{0,2,1:T(8,128)S(1)}, u32[]{:S(2)}, u32[]{:S(2)}) collective-permute-start(f32[128,3,512]{0,2,1:T(8,128)S(1)} %get-tuple-element.6), channel_id=1, source_target_pairs={{0,2},{1,3},{4,6},{5,7},{8,10},{9,11},{12,14},{13,15},{16,18},{17,... | collective-permute-start | bytes 2359304 | tf_op jit(solution)/shard_map/ppermute | solution.py:19
Sparse Core Ops, SparseCore 0:
  514.1 153.6 all-reduce.8
  753.9 127.4 reduce-scatter.1
where the time goes:
time: 961 us; the launch traced here: 947 us
  waiting for transfers between devices  333 us (35%)
  local copies, waits for them, and re-layouts  283 us (29%)
  matrix products  263 us (27%)
  other arithmetic  51.4 us (5%)
  between operations  13.6 us (1%)
    dot_general x1, matrix products, compute_power(): jnp.einsum('ctpyom,yoeq->ctpeqm', north_beams, west_table(), precision=la...  186 us
    psum x1, waiting for transfers between devices, per_device(): totals = lax.psum(jnp.sum(ordered, axis=1), 'tm')  153 us
    reduce_scatter x1, waiting for transfers between devices, per_device(): lax.psum_scatter(shift_sum(normal, delays, head_rows, out_rows), 'sub', s...  128 us
    gather x2, local copies, waits for them, and re-layouts, per_device(): jnp.take(voltages, slot_feed, axis=3)  119 us
    unnamed x5, local copies, waits for them, and re-layouts  84.4 us
    ppermute x2, waiting for transfers between devices, shifted(): lax.ppermute(value, axis, [(source, source + steps) for source in range(i...  52.1 us
    dot_general x7, matrix products, shift_sum(): jnp.einsum('ctb,cd->btd', source, onehot, preferred_element_type=jnp.floa...  49.5 us
    gather x2, local copies, waits for them, and re-layouts, per_device(): ordered = jnp.take(intensity, beam_order, axis=2)  43.4 us
  transfers between devices with their start and end apart: 4, of which 4 were waited for; matrix products, arithmetic and copies ran while one was open for 0% of the time, Pallas kernels for 0%

commit v1 on v0

--- a/solution.py
+++ b/solution.py
@@ -79,7 +79,9 @@
     )
     intensity = compute_power(north_beams)
     ordered = jnp.take(intensity, beam_order, axis=2)
-    totals = lax.psum(jnp.sum(ordered, axis=1), "tm")
+    block = jnp.sum(ordered, axis=1)
+    parts = lax.all_gather(block, "tm", axis=0, tiled=False)
+    totals = parts.sum(axis=0)
     average = totals / (sample_count * lax.axis_size("tm"))
     normal = (ordered - average[:, None, :]).astype(jnp.bfloat16)
     head_rows = 0

time: 961 us -> 1140 us (1.19)
  waiting for transfers between devices: 333 us -> 464 us
  local copies, waits for them, and re-layouts: 283 us -> 315 us
  other arithmetic: 51.4 us -> 66.1 us
    all_gather x0 -> x1, waiting for transfers between devices: none -> 284 us  [per_device(): parts = lax.all_gather(block, 'tm', axis=0, tiled=False)]
    psum x1 -> x0, waiting for transfers between devices: 153 us -> none  [per_device(): totals = lax.psum(jnp.sum(ordered, axis=1), 'tm')]
    all_gather x0 -> x1, local copies, waits for them, and re-layouts: none -> 20.4 us  [per_device(): parts = lax.all_gather(block, 'tm', axis=0, tiled=False)]
    reduce_sum x1 -> x2, other arithmetic: 8.76 us -> 23.5 us  [the longest x1 14.7 us: per_device(): totals = parts.sum(axis=0)]
    unnamed x5 -> x6, local copies, waits for them, and re-layouts: 84.4 us -> 89.7 us
where the time goes in v1:
time: 1140 us; the launch traced here: 1120 us
  waiting for transfers between devices  464 us (41%)
  local copies, waits for them, and re-layouts  315 us (28%)
  matrix products  263 us (23%)
  other arithmetic  66.1 us (6%)
  between operations  13.7 us (1%)
    all_gather x1, waiting for transfers between devices, per_device(): parts = lax.all_gather(block, 'tm', axis=0, tiled=False)  284 us
    dot_general x1, matrix products, compute_power(): jnp.einsum('ctpyom,yoeq->ctpeqm', north_beams, west_table(), precision=la...  186 us
    reduce_scatter x1, waiting for transfers between devices, per_device(): lax.psum_scatter(shift_sum(normal, delays, head_rows, out_rows), 'sub', s...  128 us
    gather x2, local copies, waits for them, and re-layouts, per_device(): jnp.take(voltages, slot_feed, axis=3)  119 us
    unnamed x6, local copies, waits for them, and re-layouts  89.7 us
    ppermute x2, waiting for transfers between devices, shifted(): lax.ppermute(value, axis, [(source, source + steps) for source in range(i...  52.1 us
    dot_general x7, matrix products, shift_sum(): jnp.einsum('ctb,cd->btd', source, onehot, preferred_element_type=jnp.floa...  49.3 us
    gather x2, local copies, waits for them, and re-layouts, per_device(): ordered = jnp.take(intensity, beam_order, axis=2)  43.4 us
  transfers between devices with their start and end apart: 4, of which 4 were waited for; matrix products, arithmetic and copies ran while one was open for 0% of the time, Pallas kernels for 0%

profile of v1, /device:TPU:24, one launch (start us, length us, event | category | flops | bytes accessed | tf_op | source)
XLA Modules:
  0.0 1123.9 jit_solution(18429372571359393546)
XLA Ops:
  11.5 84.4 %copy.50 = bf16[1024,3,2,2048]{0,1,2,3:T(4,128)(2,1)} copy(bf16[1024,3,2,2048]{3,2,1,0:T(2,128)(2,1)} %param.5) | data formatting | bytes 50331648 | tf_op args[0]
  95.8 71.0 %gather_fusion = bf16[2048,1024,3,2]{1,2,3,0:T(4,128)(2,1)} fusion(bf16[1024,3,2,2048]{0,1,2,3:T(4,128)(2,1)} %copy.50, s32[2048]{0:T(1024)S(1)} %fusion.54), kind=kCustom, calls=%fused_computation | custom fusion | bytes 50339840 | tf_op jit(solution)/shard_map/jit(_take)/gather | solution.py:74
  166.9 48.4 %copy.51 = bf16[1024,3,2,2,4,256]{5,0,2,4,3,1:T(8,128)(2,1)} copy(bf16[1024,3,2,2,4,256]{0,1,2,5,4,3:T(4,128)(2,1)} %bitcast.100) | data formatting | bytes 50331648 | tf_op jit(solution)/shard_map/jit(_take)/gather | solution.py:74
  215.6 27.5 %fusion.8 = f32[1024,3,2,4,2,256]{5,0,4,3,2,1:T(8,128)} fusion(bf16[1024,3,2,2,4,256]{5,0,2,4,3,1:T(8,128)(2,1)} %copy.51, pred[2,4,256]{2,1,0:T(4,128)(4,1)S(1)} %broadcast_in_dim.34, bf16[1,256,2,256]{3,1,0,2:T(8,128)(2,1)S(1)} %get-tuple-element.8, bf16[1,256,2,256]{3,1,0,2:T(8,128)(2,1)S(1)} %get-tuple-element.7), kind=kOutput, calls=%fused_computation.11 | convolution fusion | flops 12898533376 | bytes 76023808 | tf_op jit(solution)/shard_map/ctrpyn,rnom->ctpyom/dot_general | solution.py:77
  243.0 186.2 %fusion = f32[4,1024,3,256]{3,0,2,1:T(4,128)} fusion(f32[1024,3,2,4,2,256]{5,0,4,3,2,1:T(8,128)} %fusion.8, f32[4,2,4,2,1,1,1]{0,2,1,6,5,4,3:T(4,128)S(1)} %fusion.107), kind=kOutput, calls=%fused_computation.3 | convolution fusion | flops 1229979648 | bytes 62914816 | tf_op jit(solution)/shard_map/ctpyom,yoeq->ctpeqm/dot_general | solution.py:44
  429.2 14.6 %copy.54 = f32[1024,3,4,256]{0,3,2,1:T(8,128)} copy(f32[1024,3,4,256]{3,2,1,0:T(4,128)} %bitcast.102) | data formatting | bytes 25165824 | tf_op jit(solution)/shard_map/reduce_sum | solution.py:47
  443.8 18.1 %copy.55 = f32[1024,3,1024]{0,1,2:T(4,128)} copy(f32[1024,3,1024]{0,2,1:T(8,128)} %bitcast.101) | data formatting | bytes 25165824 | tf_op jit(solution)/shard_map/reshape | solution.py:48
  461.9 26.0 %gather_fusion.1 = f32[1024,1024,3]{1,2,0:T(4,128)} fusion(f32[1024,3,1024]{0,1,2:T(4,128)} %copy.55, s32[1024]{0:T(1024)S(1)} %fusion.56), kind=kCustom, calls=%fused_computation.1 | custom fusion | bytes 25169920 | tf_op jit(solution)/shard_map/jit(_take)/gather | solution.py:81
  487.9 17.4 %copy.56 = f32[1024,1024,3]{0,1,2:T(8,128)} copy(f32[1024,1024,3]{1,2,0:T(4,128)} %gather_fusion.1) | data formatting | bytes 25165824 | tf_op jit(solution)/shard_map/jit(_take)/gather | solution.py:81
  505.3 8.8 bitcast_reduce_fusion
  520.2 284.1 %all-gather.3.cloned.1.call-done = f32[4096,1024]{0,1:T(8,128)} async-done(((f32[1024,1024]{0,1:T(8,128)}), f32[4096,1024]{0,1:T(8,128)}) %all-gather.3.cloned.1.call-update) | async-done | bytes 16777232 | tf_op jit(solution)/shard_map/all_gather | solution.py:83
  804.3 20.4 %reshape.216 = f32[4,1024,1024]{1,0,2:T(4,128)} reshape(f32[4096,1024]{0,1:T(8,128)} %all-gather.3.cloned.1.call-done) | data formatting | bytes 33554432 | tf_op jit(solution)/shard_map/all_gather | solution.py:83
  824.7 14.7 %reduce_sum.32 = f32[1024,1024]{0,1:T(8,128)} reduce(f32[4,1024,1024]{1,0,2:T(4,128)} %reshape.216, f32[]{:T(128)} %constant.104.clone.1), dimensions={0}, to_apply=%region_2.3 | reduce | flops 3145728 | bytes 20971524 | tf_op jit(solution)/shard_map/reduce_sum | solution.py:84
  850.0 10.9 fusion.11
  861.0 7.8 convolution_bitcast_fusion.1
  873.8 7.6 convolution_bitcast_fusion.3
  881.4 7.3 convolution_bitcast_fusion.4
  888.7 7.2 convolution_bitcast_fusion.5
  895.9 7.1 convolution_bitcast_fusion.6
  903.0 7.3 convolution_bitcast_fusion
  910.3 20.4 %pad_add_fusion = f32[1024,9,512]{0,2,1:T(8,128)} fusion(f32[1024,3,512]{0,2,1:T(8,128)} %convolution_bitcast_fusion, f32[1024,3,512]{0,2,1:T(8,128)S(1)} %convolution_bitcast_fusion.1, f32[1024,3,512]{0,2,1:T(8,128)S(1)} %convolution_bitcast_fusion.2, f32[1024,3,512]{0,2,1:T(8,128)} %convolution_bitcast_fusion.3, ...), kind=kLoop, calls=%fused_computation.12 | loop fusion | flops 28311552 | bytes 62914560 | tf_op jit(solution)/shard_map/add | solution.py:66
  930.7 127.6 %reduce-scatter.2.cloned.1.call-done = f32[128,9,512]{0,2,1:T(8,128)} async-done(((f32[1024,9,512]{0,2,1:T(8,128)}), f32[128,9,512]{0,2,1:T(8,128)}) %reduce-scatter.2.cloned.1.call-update) | async-done | bytes 2359312 | tf_op jit(solution)/shard_map/reduce_scatter | solution.py:92
  1062.4 18.8 %collective-permute-done = f32[128,3,512]{0,2,1:T(8,128)S(1)} collective-permute-done((f32[128,3,512]{0,2,1:T(8,128)S(1)}, f32[128,3,512]{0,2,1:T(8,128)S(1)}, u32[]{:S(2)}, u32[]{:S(2)}) %collective-permute-start) | collective-permute-done | bytes 786464 | tf_op jit(solution)/shard_map/ppermute | solution.py:19
  1081.2 33.3 %collective-permute-done.1 = f32[128,3,512]{0,2,1:T(8,128)S(1)} collective-permute-done((f32[128,3,512]{0,2,1:T(8,128)S(1)}, f32[128,3,512]{0,2,1:T(8,128)S(1)}, u32[]{:S(2)}, u32[]{:S(2)}) %collective-permute-start.1) | collective-permute-done | bytes 786464 | tf_op jit(solution)/shard_map/ppermute | solution.py:19
  (32 shorter events, 33.3 us)
Async XLA Ops:
  6.5 797.7 %all-gather.3.cloned.1.call-start = ((), (), s32[]{:S(2)}) async-start(), calls=%async_computation.2 | async-start | bytes 20971520 | tf_op jit(solution)/shard_map/all_gather | solution.py:83
  519.4 538.9 %reduce-scatter.2.cloned.1.call-start = ((), (), s32[]{:S(2)}) async-start(), calls=%async_computation.1 | async-start | bytes 21233664 | tf_op jit(solution)/shard_map/reduce_scatter | solution.py:92
  850.0 11.0 copy-start.1
  861.0 7.8 copy-start
  1059.8 21.4 %collective-permute-start = (f32[128,3,512]{0,2,1:T(8,128)S(1)}, f32[128,3,512]{0,2,1:T(8,128)S(1)}, u32[]{:S(2)}, u32[]{:S(2)}) collective-permute-start(f32[128,3,512]{0,2,1:T(8,128)S(1)} %get-tuple-element.5), channel_id=1, source_target_pairs={{0,1},{1,2},{2,3},{4,5},{5,6},{6,7},{8,9},{9,10},{10,11},{12,13},{... | collective-permute-start | bytes 2359304 | tf_op jit(solution)/shard_map/ppermute | solution.py:19
  1061.1 53.4 %collective-permute-start.1 = (f32[128,3,512]{0,2,1:T(8,128)S(1)}, f32[128,3,512]{0,2,1:T(8,128)S(1)}, u32[]{:S(2)}, u32[]{:S(2)}) collective-permute-start(f32[128,3,512]{0,2,1:T(8,128)S(1)} %get-tuple-element.6), channel_id=1, source_target_pairs={{0,2},{1,3},{4,6},{5,7},{8,10},{9,11},{12,14},{13,15},{16,18},{17,... | collective-permute-start | bytes 2359304 | tf_op jit(solution)/shard_map/ppermute | solution.py:19
Sparse Core Ops, SparseCore 0:
  519.6 284.6 all-gather.2
  930.8 127.4 reduce-scatter.1
